TPU v7x, 32 devices: a whole 2x2x4 slice. The times are simulated.
32 devices in a mesh: seq: 32 (over z, y, x, core).
Axes of the slice: x: 2, y: 2, z: 4, core: 2. Of those that a mesh axis runs over, the one named last changes fastest.
Arguments:
- hidden: bfloat16 [4096, 2048], P('seq'), may hold values from -6 to 6
- queries: bfloat16 [4096, 2048], P('seq'), may hold values from -6 to 6
- key_rows: bfloat16 [4096, 512], P('seq'), may hold values from -6 to 6
- grad_out: bfloat16 [4096, 2048], P('seq'), may hold values from -6 to 6
- master_value: float32 [2048, 512], P('seq'), may hold values from -0.125 to 0.125
- adam_first: float32 [2048, 512], P('seq'), may hold values from -12 to 12
- adam_second: float32 [2048, 512], P('seq'), may hold values from 1 to 100
Outputs:
- attention: bfloat16 [4096, 2048], P('seq')
- grad_queries: bfloat16 [4096, 2048], P('seq')
- grad_keys: bfloat16 [4096, 512], P('seq')
- grad_hidden: bfloat16 [4096, 2048], P('seq')
- new_master: float32 [2048, 512], P('seq')
- new_first: float32 [2048, 512], P('seq')
- new_second: float32 [2048, 512], P('seq')
All inputs are finite; a program needn't handle non-finite values.
Results may differ from a plain program's by a relative error of at most 0.02.
Values may be sent and summed in bfloat16 or wider, within the bound.
No kernel may reach another device: no remote copies, remote signals or barrier semaphores. Data moves between devices by JAX's collectives and lax.ppermute only.
A program may use at most 64 MiB of HBM per device.

v0:
```python
import math
import jax
import jax.numpy as jnp
from jax import lax
from jax.sharding import PartitionSpec as P

HQ = 16
HK = 4
DH = 128
WINDOW = 512
OPT_STEP = 10
beta_first = 0.9
beta_second = 0.95
learning = 0.001
decay_rate = 0.1
epsilon = 1e-08


def passed_along(block, axis, distance):
    devices = range(lax.axis_size(axis))
    route = [(i - distance, i) for i in devices if i - distance in devices]
    return lax.ppermute(block, axis, route)


def attend_block(query_blk, grad_blk, key_win, value_win, allowed):
    ratio = HQ // HK
    scale = 1.0 / math.sqrt(DH)
    count = query_blk.shape[0]
    out_parts, dq_parts, dk_parts, dv_parts = ([], [], [], [])
    for group in range(HK):
        low = group * ratio * DH
        high = (group + 1) * ratio * DH
        query_group = query_blk[:, low:high].reshape(count, ratio, DH)
        grad_group = grad_blk[:, low:high].reshape(count, ratio, DH)
        key_group = key_win[:, group * DH : (group + 1) * DH]
        value_group = value_win[:, group * DH : (group + 1) * DH]
        scores = (
            jnp.einsum("trd,sd->trs", query_group, key_group, preferred_element_type=jnp.float32)
            * scale
        )
        scores = jnp.where(allowed[:, None, :], scores, -jnp.inf)
        top = jnp.max(scores, axis=2, keepdims=True)
        expd = jnp.exp(scores - top)
        probs = expd / jnp.sum(expd, axis=2, keepdims=True)
        probs_low = probs.astype(jnp.bfloat16)
        out_group = jnp.einsum(
            "trs,sd->trd", probs_low, value_group, preferred_element_type=jnp.float32
        ).astype(jnp.bfloat16)
        delta = jnp.sum(
            grad_group.astype(jnp.float32) * out_group.astype(jnp.float32), axis=2, keepdims=True
        )
        dprob = jnp.einsum(
            "trd,sd->trs", grad_group, value_group, preferred_element_type=jnp.float32
        )
        dscore = (probs * (dprob - delta)).astype(jnp.bfloat16)
        dq_group = (
            jnp.einsum("trs,sd->trd", dscore, key_group, preferred_element_type=jnp.float32) * scale
        ).astype(jnp.bfloat16)
        dk_group = (
            jnp.einsum("trs,trd->sd", dscore, query_group, preferred_element_type=jnp.float32)
            * scale
        )
        dv_group = jnp.einsum(
            "trs,trd->sd", probs_low, grad_group, preferred_element_type=jnp.float32
        )
        out_parts.append(out_group.reshape(count, ratio * DH))
        dq_parts.append(dq_group.reshape(count, ratio * DH))
        dk_parts.append(dk_group)
        dv_parts.append(dv_group)
    return (
        jnp.concatenate(out_parts, 1),
        jnp.concatenate(dq_parts, 1),
        jnp.concatenate(dk_parts, 1),
        jnp.concatenate(dv_parts, 1),
    )


def shards(hidden, queries, key_rows, grad_out, master_value, adam_first, adam_second):
    tok_rows = hidden.shape[0]
    reach = WINDOW // tok_rows
    position = lax.axis_index("seq")
    weight_low = master_value.astype(jnp.bfloat16)
    weight_full = lax.all_gather(weight_low, "seq", axis=0, tiled=True)
    values = jnp.dot(hidden, weight_full, preferred_element_type=jnp.float32).astype(jnp.bfloat16)
    earlier = []
    for distance in range(1, reach + 1):
        earlier.append(passed_along((key_rows, values), "seq", distance))
    ordered = earlier[::-1]
    key_win = jnp.concatenate([entry[0] for entry in ordered] + [key_rows], 0)
    value_win = jnp.concatenate([entry[1] for entry in ordered] + [values], 0)
    span_rows = (reach + 1) * tok_rows
    key_index = jnp.arange(span_rows, dtype=jnp.int32)
    key_pos = position * tok_rows - WINDOW + key_index
    relative = jnp.arange(tok_rows, dtype=jnp.int32)[:, None] + WINDOW - key_index[None, :]
    allowed = (relative >= 0) & (relative < WINDOW) & (key_pos >= 0)[None, :]
    attention, grad_queries, dk_win, dv_win = attend_block(
        queries, grad_out, key_win, value_win, allowed
    )

    def partial_terms(distance):
        low = (reach - distance) * tok_rows
        return (dk_win[low : low + tok_rows], dv_win[low : low + tok_rows])

    key_total, value_total = partial_terms(0)
    for distance in range(1, reach + 1):
        arrived = passed_along(partial_terms(distance), "seq", -distance)
        key_total = key_total + arrived[0]
        value_total = value_total + arrived[1]
    grad_keys = key_total.astype(jnp.bfloat16)
    d_value = value_total.astype(jnp.bfloat16)
    grad_hidden = lax.dot_general(
        d_value, weight_full, (((1,), (1,)), ((), ())), preferred_element_type=jnp.float32
    ).astype(jnp.bfloat16)
    grad_weight = lax.psum_scatter(
        lax.dot_general(
            hidden, d_value, (((0,), (0,)), ((), ())), preferred_element_type=jnp.float32
        ),
        "seq",
        scatter_dimension=0,
        tiled=True,
    )
    new_first = beta_first * adam_first + (1.0 - beta_first) * grad_weight
    new_second = beta_second * adam_second + (1.0 - beta_second) * grad_weight * grad_weight
    first_hat = new_first / (1.0 - beta_first**OPT_STEP)
    second_hat = new_second / (1.0 - beta_second**OPT_STEP)
    new_master = master_value - learning * (
        first_hat / (jnp.sqrt(second_hat) + epsilon) + decay_rate * master_value
    )
    return (attention, grad_queries, grad_keys, grad_hidden, new_master, new_first, new_second)


def solution(mesh):
    placed = (
        P("seq", None),
        P("seq", None),
        P("seq", None),
        P("seq", None),
        P("seq", None),
        P("seq", None),
        P("seq", None),
    )
    return jax.shard_map(
        shards,
        mesh=mesh,
        in_specs=placed,
        out_specs=(
            P("seq", None),
            P("seq", None),
            P("seq", None),
            P("seq", None),
            P("seq", None),
            P("seq", None),
            P("seq", None),
        ),
        check_vma=False,
    )
```

profile of v0, /device:TPU:6, one launch (start us, length us, event | category | flops | bytes accessed | tf_op | source)
XLA Modules:
  0.0 334.3 jit_solution(691577577510038583)
XLA Ops:
  7.2 3.5 %collective-permute-start.2 = (bf16[128,512]{1,0:T(8,128)(2,1)}, bf16[128,512]{1,0:T(8,128)(2,1)S(1)}, u32[]{:S(2)}, u32[]{:S(2)}) collective-permute-start(bf16[128,512]{1,0:T(8,128)(2,1)} %param.9), channel_id=1, source_target_pairs={{0,2},{1,3},{2,4},{3,5},{4,6},{5,7},{6,8},{7,9},{8,10},{9,11},{10,... | collective-permute-start | bytes 393224 | tf_op jit(solution)/shard_map/ppermute | solution.py:22
  10.8 2.6 collective-permute-start.1
  13.3 3.4 %collective-permute-start = (bf16[128,512]{1,0:T(8,128)(2,1)}, bf16[128,512]{1,0:T(8,128)(2,1)S(1)}, u32[]{:S(2)}, u32[]{:S(2)}) collective-permute-start(bf16[128,512]{1,0:T(8,128)(2,1)} %param.9), channel_id=1, source_target_pairs={{0,4},{1,5},{2,6},{3,7},{4,8},{5,9},{6,10},{7,11},{8,12},{9,13},{1... | collective-permute-start | bytes 393224 | tf_op jit(solution)/shard_map/ppermute | solution.py:22
  16.8 2.6 collective-permute-start.3
  19.4 1.1 fusion.73
  20.6 0.8 fusion.47
  22.4 0.8 copy.206
  23.3 0.8 copy-done.27
  24.2 1.5 fusion.74
  25.7 2.7 fusion.76
  28.4 2.5 fusion.75
  30.9 2.5 fusion.77
  33.8 0.8 copy-done.4
  35.2 0.8 copy-done.6
  36.5 0.8 copy-done.2
  38.0 2.9 collective-permute-start.12
  40.9 2.4 collective-permute-start.15
  43.3 1.9 collective-permute-start.14
  45.2 2.9 collective-permute-start.13
  48.1 11.6 %collective-permute-done.15 = f32[128,512]{0,1:T(8,128)S(1)} collective-permute-done((f32[128,512]{0,1:T(8,128)S(1)}, f32[128,512]{0,1:T(8,128)S(1)}, u32[]{:S(2)}, u32[]{:S(2)}) %collective-permute-start.15) | collective-permute-done | bytes 262176 | tf_op jit(solution)/shard_map/ppermute | solution.py:22
  59.7 2.8 collective-permute-done.14
  62.5 2.9 collective-permute-done.13
  65.4 2.7 convolution_bitcast_fusion
  68.2 5.3 %copy.270 = f32[2048,512]{1,0:T(8,128)} copy(f32[2048,512]{0,1:T(8,128)} %convolution_bitcast_fusion) | data formatting | bytes 8388608
  73.6 127.5 %reduce-scatter.4.cloned.1.call-done = f32[64,512]{1,0:T(8,128)} async-done(((f32[2048,512]{1,0:T(8,128)}), f32[64,512]{1,0:T(8,128)}) %reduce-scatter.4.cloned.1.call-update) | async-done | bytes 131088 | tf_op jit(solution)/shard_map/reduce_scatter | solution.py:114
  201.0 2.0 multiply_subtract_fusion
  203.0 67.2 %all-gather.2.cloned.1.call-done = bf16[2048,512]{1,0:T(8,128)(2,1)} async-done(((bf16[64,512]{1,0:T(8,128)(2,1)}), bf16[2048,512]{1,0:T(8,128)(2,1)}) %all-gather.2.cloned.1.call-update) | async-done | bytes 2097168 | tf_op jit(solution)/shard_map/all_gather | solution.py:83
  270.2 2.2 convolution_convert_fusion.5
  272.4 2.1 collective-permute-start.7
  274.6 3.3 collective-permute-start.6
  277.9 4.1 %collective-permute-start.5 = (bf16[128,512]{1,0:T(8,128)(2,1)S(1)}, bf16[128,512]{1,0:T(8,128)(2,1)S(1)}, u32[]{:S(2)}, u32[]{:S(2)}) collective-permute-start(bf16[128,512]{1,0:T(8,128)(2,1)S(1)} %convolution_convert_fusion.5), channel_id=1, source_target_pairs={{0,3},{1,4},{2,5},{3,6},{4,7},{5,8},{6,9},{7,10},{8,11},{9,12},{10... | collective-permute-start | bytes 393224 | tf_op jit(solution)/shard_map/ppermute | solution.py:22
  282.0 2.7 collective-permute-start.4
  284.6 1.6 convolution_convert_fusion
  286.3 2.6 collective-permute-done.4
  289.0 1.0 multiply_reduce_fusion
  292.0 0.7 copy-done.28
  296.0 1.0 fusion.37
  298.2 1.0 fusion.71
  299.2 2.7 collective-permute-start.8
  302.0 1.9 collective-permute-start.11
  303.9 1.9 collective-permute-start.10
  305.8 2.8 collective-permute-start.9
  310.0 1.1 pad_maximum_fusion.2
  311.1 9.3 %collective-permute-done.11 = f32[128,512]{0,1:T(8,128)S(1)} collective-permute-done((f32[128,512]{0,1:T(8,128)}, f32[128,512]{0,1:T(8,128)S(1)}, u32[]{:S(2)}, u32[]{:S(2)}) %collective-permute-start.11) | collective-permute-done | bytes 262176 | tf_op jit(solution)/shard_map/ppermute | solution.py:22
  320.4 2.8 collective-permute-done.10
  323.2 2.4 collective-permute-done.9
  325.6 1.1 fusion.55
  326.7 0.8 copy.229
  (120 shorter events, 10.9 us)
Async XLA Ops:
  7.2 58.3 %copy-start = (bf16[128,2048]{1,0:T(8,128)(2,1)S(1)}, bf16[128,2048]{1,0:T(8,128)(2,1)}, u32[]{:S(2)}) copy-start(bf16[128,2048]{1,0:T(8,128)(2,1)} %param.7) | copy-start | bytes 1572868
  7.2 13.4 %copy-start.22 = (bf16[128,2048]{1,0:T(8,128)(2,1)S(1)}, bf16[128,2048]{1,0:T(8,128)(2,1)}, u32[]{:S(2)}) copy-start(bf16[128,2048]{1,0:T(8,128)(2,1)} %param.10) | copy-start | bytes 1572868
  7.2 193.8 %reduce-scatter.4.cloned.1.call-start = ((), (), s32[]{:S(2)}) async-start(), calls=%async_computation.2 | async-start | bytes 4325376 | tf_op jit(solution)/shard_map/reduce_scatter | solution.py:114
  7.2 16.0 %collective-permute-start.2 = (bf16[128,512]{1,0:T(8,128)(2,1)}, bf16[128,512]{1,0:T(8,128)(2,1)S(1)}, u32[]{:S(2)}, u32[]{:S(2)}) collective-permute-start(bf16[128,512]{1,0:T(8,128)(2,1)} %param.9), channel_id=1, source_target_pairs={{0,2},{1,3},{2,4},{3,5},{4,6},{5,7},{6,8},{7,9},{8,10},{9,11},{10,... | collective-permute-start | bytes 393224 | tf_op jit(solution)/shard_map/ppermute | solution.py:22
  10.8 12.4 %collective-permute-start.1 = (bf16[128,512]{1,0:T(8,128)(2,1)}, bf16[128,512]{1,0:T(8,128)(2,1)S(1)}, u32[]{:S(2)}, u32[]{:S(2)}) collective-permute-start(bf16[128,512]{1,0:T(8,128)(2,1)} %param.9), channel_id=1, source_target_pairs={{0,3},{1,4},{2,5},{3,6},{4,7},{5,8},{6,9},{7,10},{8,11},{9,12},{10... | collective-permute-start | bytes 393224 | tf_op jit(solution)/shard_map/ppermute | solution.py:22
  13.3 9.8 %collective-permute-start = (bf16[128,512]{1,0:T(8,128)(2,1)}, bf16[128,512]{1,0:T(8,128)(2,1)S(1)}, u32[]{:S(2)}, u32[]{:S(2)}) collective-permute-start(bf16[128,512]{1,0:T(8,128)(2,1)} %param.9), channel_id=1, source_target_pairs={{0,4},{1,5},{2,6},{3,7},{4,8},{5,9},{6,10},{7,11},{8,12},{9,13},{1... | collective-permute-start | bytes 393224 | tf_op jit(solution)/shard_map/ppermute | solution.py:22
  16.8 6.5 %collective-permute-start.3 = (bf16[128,512]{1,0:T(8,128)(2,1)}, bf16[128,512]{1,0:T(8,128)(2,1)S(1)}, u32[]{:S(2)}, u32[]{:S(2)}) collective-permute-start(bf16[128,512]{1,0:T(8,128)(2,1)} %param.9), channel_id=1, source_target_pairs={{0,1},{1,2},{2,3},{3,4},{4,5},{5,6},{6,7},{7,8},{8,9},{9,10},{10,1... | collective-permute-start | bytes 393224 | tf_op jit(solution)/shard_map/ppermute | solution.py:22
  21.7 6.7 %copy-start.12 = (bf16[128,512]{0,1:T(8,128)(2,1)}, bf16[128,512]{0,1:T(8,128)(2,1)S(1)}, u32[]{:S(2)}) copy-start(bf16[128,512]{0,1:T(8,128)(2,1)S(1)} %copy.274) | copy-start | bytes 393220
  21.7 1.6 copy-start.23
  21.8 2.4 copy-start.26
  22.0 3.7 %copy-start.16 = (bf16[128,512]{0,1:T(8,128)(2,1)}, bf16[128,512]{0,1:T(8,128)(2,1)S(1)}, u32[]{:S(2)}) copy-start(bf16[128,512]{0,1:T(8,128)(2,1)S(1)} %copy.275) | copy-start | bytes 393220
  22.1 15.3 %copy-start.10 = (bf16[128,512]{0,1:T(8,128)(2,1)}, bf16[128,512]{0,1:T(8,128)(2,1)S(1)}, u32[]{:S(2)}) copy-start(bf16[128,512]{0,1:T(8,128)(2,1)S(1)} %copy.198) | copy-start | bytes 393220
  22.2 12.6 %copy-start.14 = (bf16[128,512]{0,1:T(8,128)(2,1)}, bf16[128,512]{0,1:T(8,128)(2,1)S(1)}, u32[]{:S(2)}) copy-start(bf16[128,512]{0,1:T(8,128)(2,1)S(1)} %copy.202) | copy-start | bytes 393220
  22.4 11.1 %copy-start.20 = (bf16[128,512]{0,1:T(8,128)(2,1)}, bf16[128,512]{0,1:T(8,128)(2,1)S(1)}, u32[]{:S(2)}) copy-start(bf16[128,512]{0,1:T(8,128)(2,1)S(1)} %copy.210) | copy-start | bytes 393220
  23.3 0.9 copy-start.27
  25.7 7.7 %copy-start.8 = (f32[128,4,640]{0,2,1:T(8,128)}, f32[128,4,640]{0,2,1:T(8,128)S(1)}, u32[]{:S(2)}) copy-start(f32[128,4,640]{0,2,1:T(8,128)S(1)} %get-tuple-element.56) | copy-start | bytes 3932164
  33.4 1.3 copy-start.4
  34.7 1.3 copy-start.6
  34.8 1.3 copy-start.18
  36.0 1.3 copy-start.2
  38.0 10.1 %collective-permute-start.12 = (f32[128,512]{0,1:T(8,128)S(1)}, f32[128,512]{0,1:T(8,128)S(1)}, u32[]{:S(2)}, u32[]{:S(2)}) collective-permute-start(f32[128,512]{0,1:T(8,128)S(1)} %get-tuple-element.38), channel_id=1, source_target_pairs={{1,0},{2,1},{3,2},{4,3},{5,4},{6,5},{7,6},{8,7},{9,8},{10,9},{11,1... | collective-permute-start | bytes 786440 | tf_op jit(solution)/shard_map/ppermute | solution.py:22
  40.9 18.8 %collective-permute-start.15 = (f32[128,512]{0,1:T(8,128)S(1)}, f32[128,512]{0,1:T(8,128)S(1)}, u32[]{:S(2)}, u32[]{:S(2)}) collective-permute-start(f32[128,512]{0,1:T(8,128)S(1)} %get-tuple-element.39), channel_id=1, source_target_pairs={{4,0},{5,1},{6,2},{7,3},{8,4},{9,5},{10,6},{11,7},{12,8},{13,9},{1... | collective-permute-start | bytes 786440 | tf_op jit(solution)/shard_map/ppermute | solution.py:22
  43.3 19.2 %collective-permute-start.14 = (f32[128,512]{0,1:T(8,128)S(1)}, f32[128,512]{0,1:T(8,128)S(1)}, u32[]{:S(2)}, u32[]{:S(2)}) collective-permute-start(f32[128,512]{0,1:T(8,128)S(1)} %get-tuple-element.40), channel_id=1, source_target_pairs={{3,0},{4,1},{5,2},{6,3},{7,4},{8,5},{9,6},{10,7},{11,8},{12,9},{13... | collective-permute-start | bytes 786440 | tf_op jit(solution)/shard_map/ppermute | solution.py:22
  45.2 20.1 %collective-permute-start.13 = (f32[128,512]{0,1:T(8,128)S(1)}, f32[128,512]{0,1:T(8,128)S(1)}, u32[]{:S(2)}, u32[]{:S(2)}) collective-permute-start(f32[128,512]{0,1:T(8,128)S(1)} %get-tuple-element.41), channel_id=1, source_target_pairs={{2,0},{3,1},{4,2},{5,3},{6,4},{7,5},{8,6},{9,7},{10,8},{11,9},{12,... | collective-permute-start | bytes 786440 | tf_op jit(solution)/shard_map/ppermute | solution.py:22
  73.5 196.7 %all-gather.2.cloned.1.call-start = ((), (), s32[]{:S(2)}) async-start(), calls=%async_computation.1 | async-start | bytes 2162688 | tf_op jit(solution)/shard_map/all_gather | solution.py:83
  270.2 14.4 %copy-start.1 = (bf16[2048,512]{1,0:T(8,128)(2,1)S(1)}, bf16[2048,512]{1,0:T(8,128)(2,1)}, u32[]{:S(2)}) copy-start(bf16[2048,512]{1,0:T(8,128)(2,1)} %all-gather.2.cloned.1.call-done) | copy-start | bytes 6291460
  272.4 16.5 %collective-permute-start.7 = (bf16[128,512]{1,0:T(8,128)(2,1)S(1)}, bf16[128,512]{1,0:T(8,128)(2,1)S(1)}, u32[]{:S(2)}, u32[]{:S(2)}) collective-permute-start(bf16[128,512]{1,0:T(8,128)(2,1)S(1)} %convolution_convert_fusion.5), channel_id=1, source_target_pairs={{0,1},{1,2},{2,3},{3,4},{4,5},{5,6},{6,7},{7,8},{8,9},{9,10},{10,1... | collective-permute-start | bytes 393224 | tf_op jit(solution)/shard_map/ppermute | solution.py:22
  274.6 14.3 %collective-permute-start.6 = (bf16[128,512]{1,0:T(8,128)(2,1)S(1)}, bf16[128,512]{1,0:T(8,128)(2,1)S(1)}, u32[]{:S(2)}, u32[]{:S(2)}) collective-permute-start(bf16[128,512]{1,0:T(8,128)(2,1)S(1)} %convolution_convert_fusion.5), channel_id=1, source_target_pairs={{0,2},{1,3},{2,4},{3,5},{4,6},{5,7},{6,8},{7,9},{8,10},{9,11},{10,... | collective-permute-start | bytes 393224 | tf_op jit(solution)/shard_map/ppermute | solution.py:22
  277.9 10.9 %collective-permute-start.5 = (bf16[128,512]{1,0:T(8,128)(2,1)S(1)}, bf16[128,512]{1,0:T(8,128)(2,1)S(1)}, u32[]{:S(2)}, u32[]{:S(2)}) collective-permute-start(bf16[128,512]{1,0:T(8,128)(2,1)S(1)} %convolution_convert_fusion.5), channel_id=1, source_target_pairs={{0,3},{1,4},{2,5},{3,6},{4,7},{5,8},{6,9},{7,10},{8,11},{9,12},{10... | collective-permute-start | bytes 393224 | tf_op jit(solution)/shard_map/ppermute | solution.py:22
  282.0 6.9 %collective-permute-start.4 = (bf16[128,512]{1,0:T(8,128)(2,1)S(1)}, bf16[128,512]{1,0:T(8,128)(2,1)S(1)}, u32[]{:S(2)}, u32[]{:S(2)}) collective-permute-start(bf16[128,512]{1,0:T(8,128)(2,1)S(1)} %convolution_convert_fusion.5), channel_id=1, source_target_pairs={{0,4},{1,5},{2,6},{3,7},{4,8},{5,9},{6,10},{7,11},{8,12},{9,13},{1... | collective-permute-start | bytes 393224 | tf_op jit(solution)/shard_map/ppermute | solution.py:22
  286.3 2.7 copy-start.21
  286.3 3.7 %copy-start.19 = (bf16[128,512]{0,1:T(8,128)(2,1)S(1)}, bf16[128,512]{0,1:T(8,128)(2,1)}, u32[]{:S(2)}) copy-start(bf16[128,512]{0,1:T(8,128)(2,1)} %copy.206) | copy-start | bytes 393220
  288.9 1.3 copy-start.15
  290.0 0.9 copy-start.11
  290.3 1.3 copy-start.9
  291.6 1.1 copy-start.28
  291.6 1.4 copy-start.17
  292.7 1.3 copy-start.7
  294.0 0.9 copy-start.13
  294.4 1.3 copy-start.5
  296.0 1.4 copy-start.3
  299.2 10.1 %copy-start.24 = (bf16[128,4,128]{0,2,1:T(8,128)(2,1)S(1)}, bf16[128,4,128]{0,2,1:T(8,128)(2,1)}, u32[]{:S(2)}) copy-start(bf16[128,4,128]{0,2,1:T(8,128)(2,1)} %get-tuple-element.64) | copy-start | bytes 393220
  299.2 11.8 %collective-permute-start.8 = (f32[128,512]{0,1:T(8,128)}, f32[128,512]{0,1:T(8,128)S(1)}, u32[]{:S(2)}, u32[]{:S(2)}) collective-permute-start(f32[128,512]{0,1:T(8,128)} %get-tuple-element.42), channel_id=1, source_target_pairs={{1,0},{2,1},{3,2},{4,3},{5,4},{6,5},{7,6},{8,7},{9,8},{10,9},{11,1... | collective-permute-start | bytes 786440 | tf_op jit(solution)/shard_map/ppermute | solution.py:22
  302.0 18.4 %collective-permute-start.11 = (f32[128,512]{0,1:T(8,128)}, f32[128,512]{0,1:T(8,128)S(1)}, u32[]{:S(2)}, u32[]{:S(2)}) collective-permute-start(f32[128,512]{0,1:T(8,128)} %get-tuple-element.43), channel_id=1, source_target_pairs={{4,0},{5,1},{6,2},{7,3},{8,4},{9,5},{10,6},{11,7},{12,8},{13,9},{1... | collective-permute-start | bytes 786440 | tf_op jit(solution)/shard_map/ppermute | solution.py:22
  303.9 19.3 %collective-permute-start.10 = (f32[128,512]{0,1:T(8,128)}, f32[128,512]{0,1:T(8,128)}, u32[]{:S(2)}, u32[]{:S(2)}) collective-permute-start(f32[128,512]{0,1:T(8,128)} %get-tuple-element.44), channel_id=1, source_target_pairs={{3,0},{4,1},{5,2},{6,3},{7,4},{8,5},{9,6},{10,7},{11,8},{12,9},{13... | collective-permute-start | bytes 786440 | tf_op jit(solution)/shard_map/ppermute | solution.py:22
  305.8 4.0 %copy-start.25 = (bf16[128,4,128]{0,2,1:T(8,128)(2,1)S(1)}, bf16[128,4,128]{0,2,1:T(8,128)(2,1)}, u32[]{:S(2)}) copy-start(bf16[128,4,128]{0,2,1:T(8,128)(2,1)} %fusion.37) | copy-start | bytes 393220
  305.8 19.8 %collective-permute-start.9 = (f32[128,512]{0,1:T(8,128)}, f32[128,512]{0,1:T(8,128)}, u32[]{:S(2)}, u32[]{:S(2)}) collective-permute-start(f32[128,512]{0,1:T(8,128)} %get-tuple-element.45), channel_id=1, source_target_pairs={{2,0},{3,1},{4,2},{5,3},{6,4},{7,5},{8,6},{9,7},{10,8},{11,9},{12,... | collective-permute-start | bytes 786440 | tf_op jit(solution)/shard_map/ppermute | solution.py:22
Sparse Core Ops, SparseCore 0:
  73.6 127.3 reduce-scatter.3
  204.5 65.7 all-gather.1
where the time goes:
time: 335 us; the launch traced here: 334 us
  waiting for transfers between devices  229 us (68%)
  starting transfers between devices  43.9 us (13%)
  matrix products  23.7 us (7%)
  local copies, waits for them, and re-layouts  17.2 us (5%)
  between operations  14.8 us (4%)
  other arithmetic  5.69 us (2%)
    reduce_scatter x1, waiting for transfers between devices, shards(): lax.psum_scatter(lax.dot_general(hidden, d_value, (((0,), (0,)), ((), ())...  127 us
    all_gather x1, waiting for transfers between devices, shards(): weight_full = lax.all_gather(weight_low, 'seq', axis=0, tiled=True)  67.2 us
    ppermute x16, starting transfers between devices, passed_along(): return lax.ppermute(block, axis, route)  43.8 us
    ppermute x16, waiting for transfers between devices, passed_along(): return lax.ppermute(block, axis, route)  34.4 us
    unnamed x72, local copies, waits for them, and re-layouts  12.8 us
    sub x4, matrix products, attend_block(): expd = jnp.exp(scores - top)  9.17 us
  transfers between devices with their start and end apart: 18, of which 10 were waited for; matrix products, arithmetic and copies ran while one was open for 2% of the time, Pallas kernels for 0%

commit v1 on v0

--- a/solution.py
+++ b/solution.py
@@ -14,6 +14,18 @@
 learning = 0.001
 decay_rate = 0.1
 epsilon = 1e-08
+
+
+def collect(x, axis, dim):
+    ways, here = (lax.axis_size(axis), lax.axis_index(axis))
+    grown, reach = (x, 1)
+    while reach < ways:
+        theirs = lax.ppermute(grown, axis, [(d, d ^ reach) for d in range(ways)])
+        mine_first = jnp.concatenate([grown, theirs], axis=dim)
+        theirs_first = jnp.concatenate([theirs, grown], axis=dim)
+        grown = jnp.where(here & reach == 0, mine_first, theirs_first)
+        reach = 2 * reach
+    return grown
 
 
 def passed_along(block, axis, distance):
@@ -80,7 +92,7 @@
     reach = WINDOW // tok_rows
     position = lax.axis_index("seq")
     weight_low = master_value.astype(jnp.bfloat16)
-    weight_full = lax.all_gather(weight_low, "seq", axis=0, tiled=True)
+    weight_full = collect(weight_low, "seq", 0)
     values = jnp.dot(hidden, weight_full, preferred_element_type=jnp.float32).astype(jnp.bfloat16)
     earlier = []
     for distance in range(1, reach + 1):

time: 335 us -> 368 us (1.099); the launches traced: 334 us -> 363 us
  starting transfers between devices: 43.9 us -> 58.5 us
  other arithmetic: 5.69 us -> 12.3 us
    ppermute x0 -> x5, waiting for transfers between devices: none -> 71.4 us  [collect(): theirs = lax.ppermute(grown, axis, [(d, d ^ reach) for d in range(ways)])]
    all_gather x1 -> x0, waiting for transfers between devices: 67.2 us -> none  [shards(): weight_full = lax.all_gather(weight_low, 'seq', axis=0, tiled=True)]
    ppermute x0 -> x5, starting transfers between devices: none -> 16.1 us  [collect(): theirs = lax.ppermute(grown, axis, [(d, d ^ reach) for d in range(ways)])]
    select_n x0 -> x4, other arithmetic: none -> 6.06 us  [collect(): grown = jnp.where(here & reach == 0, mine_first, theirs_first)]
    unnamed x72 -> x74, local copies, waits for them, and re-layouts: 12.8 us -> 13.5 us
  transfers between devices with their start and end apart: 18 -> 22, of which waited for: 10 -> 13; matrix products, arithmetic and copies ran while one was open for 2% -> 3% of each run, Pallas kernels for 0% -> 0%
where the time goes in v1:
time: 368 us; the launch traced here: 363 us
  waiting for transfers between devices  232 us (63%)
  starting transfers between devices  58.5 us (16%)
  matrix products  25.6 us (7%)
  local copies, waits for them, and re-layouts  20.3 us (6%)
  between operations  14.9 us (4%)
  other arithmetic  12.3 us (3%)
    reduce_scatter x1, waiting for transfers between devices, shards(): lax.psum_scatter(lax.dot_general(hidden, d_value, (((0,), (0,)), ((), ())...  130 us
    ppermute x5, waiting for transfers between devices, collect(): theirs = lax.ppermute(grown, axis, [(d, d ^ reach) for d in range(ways)])  71.4 us
    ppermute x16, starting transfers between devices, passed_along(): return lax.ppermute(block, axis, route)  42.4 us
    ppermute x16, waiting for transfers between devices, passed_along(): return lax.ppermute(block, axis, route)  31.1 us
    ppermute x5, starting transfers between devices, collect(): theirs = lax.ppermute(grown, axis, [(d, d ^ reach) for d in range(ways)])  16.1 us
    unnamed x74, local copies, waits for them, and re-layouts  13.5 us
    sub x4, matrix products, attend_block(): expd = jnp.exp(scores - top)  8.3 us
  transfers between devices with their start and end apart: 22, of which 13 were waited for; matrix products, arithmetic and copies ran while one was open for 3% of the time, Pallas kernels for 0%

profile of v1, /device:TPU:6, one launch (start us, length us, event | category | flops | bytes accessed | tf_op | source)
XLA Modules:
  0.0 363.5 jit_solution(18426510624071268028)
XLA Ops:
  7.2 3.6 collective-permute-start
  10.8 2.6 collective-permute-start.1
  13.4 3.4 collective-permute-start.2
  16.8 2.6 collective-permute-start.3
  19.4 1.1 fusion.76
  23.3 1.6 fusion.80
  25.0 1.5 fusion.79
  26.5 2.7 fusion.78
  29.1 2.5 fusion.77
  31.7 1.4 fusion.41
  36.8 2.9 collective-permute-start.17
  39.7 3.3 collective-permute-start.18
  43.1 1.9 collective-permute-start.19
  45.0 1.9 collective-permute-start.20
  46.9 12.0 %collective-permute-done.18 = f32[128,512]{0,1:T(8,128)S(1)} collective-permute-done((f32[128,512]{0,1:T(8,128)S(1)}, f32[128,512]{0,1:T(8,128)S(1)}, u32[]{:S(2)}, u32[]{:S(2)}) %collective-permute-start.18) | collective-permute-done | bytes 262176 | tf_op jit(solution)/shard_map/ppermute | solution.py:34
  59.0 2.5 collective-permute-done.19
  61.5 2.7 collective-permute-done.20
  64.9 2.7 convolution_bitcast_fusion
  67.6 5.3 %copy.270 = f32[2048,512]{1,0:T(8,128)} copy(f32[2048,512]{0,1:T(8,128)} %convolution_bitcast_fusion) | data formatting | bytes 8388608
  73.0 129.5 %reduce-scatter.4.cloned.1.call-done = f32[64,512]{1,0:T(8,128)} async-done(((f32[2048,512]{1,0:T(8,128)}), f32[64,512]{1,0:T(8,128)}) %reduce-scatter.4.cloned.1.call-update) | async-done | bytes 131088 | tf_op jit(solution)/shard_map/reduce_scatter | solution.py:126
  202.5 1.8 multiply_subtract_fusion
  204.4 1.3 collective-permute-done.4
  205.7 5.5 %collective-permute-start.5 = (bf16[128,512]{1,0:T(8,128)(2,1)S(1)}, bf16[128,512]{1,0:T(8,128)(2,1)}, u32[]{:S(2)}, u32[]{:S(2)}) collective-permute-start(bf16[128,512]{1,0:T(8,128)(2,1)S(1)} %maximum_select_fusion.6), channel_id=1, source_target_pairs={{0,2},{1,3},{2,0},{3,1},{4,6},{5,7},{6,4},{7,5},{8,10},{9,11},{10,... | collective-permute-start | bytes 393224 | tf_op jit(solution)/shard_map/ppermute | solution.py:23
  211.2 3.9 %collective-permute-done.5 = bf16[128,512]{1,0:T(8,128)(2,1)} collective-permute-done((bf16[128,512]{1,0:T(8,128)(2,1)S(1)}, bf16[128,512]{1,0:T(8,128)(2,1)}, u32[]{:S(2)}, u32[]{:S(2)}) %collective-permute-start.5) | collective-permute-done | bytes 131104 | tf_op jit(solution)/shard_map/ppermute | solution.py:23
  215.1 1.2 maximum_select_fusion.5
  216.3 10.5 %collective-permute-start.6 = (bf16[256,512]{1,0:T(8,128)(2,1)S(1)}, bf16[256,512]{1,0:T(8,128)(2,1)}, u32[]{:S(2)}, u32[]{:S(2)}) collective-permute-start(bf16[256,512]{1,0:T(8,128)(2,1)S(1)} %maximum_select_fusion.5), channel_id=1, source_target_pairs={{0,4},{1,5},{2,6},{3,7},{4,0},{5,1},{6,2},{7,3},{8,12},{9,13},{10,... | collective-permute-start | bytes 786440 | tf_op jit(solution)/shard_map/ppermute | solution.py:23
  226.8 6.2 %collective-permute-done.6 = bf16[256,512]{1,0:T(8,128)(2,1)} collective-permute-done((bf16[256,512]{1,0:T(8,128)(2,1)S(1)}, bf16[256,512]{1,0:T(8,128)(2,1)}, u32[]{:S(2)}, u32[]{:S(2)}) %collective-permute-start.6) | collective-permute-done | bytes 262176 | tf_op jit(solution)/shard_map/ppermute | solution.py:23
  233.0 2.0 maximum_select_fusion.2
  234.9 13.1 %collective-permute-done.7 = bf16[512,512]{1,0:T(8,128)(2,1)} collective-permute-done((bf16[512,512]{1,0:T(8,128)(2,1)}, bf16[512,512]{1,0:T(8,128)(2,1)}, u32[]{:S(2)}, u32[]{:S(2)}) %collective-permute-start.7) | collective-permute-done | bytes 524320 | tf_op jit(solution)/shard_map/ppermute | solution.py:23
  248.1 2.9 maximum_select_fusion.1
  251.0 46.9 %collective-permute-done.8 = bf16[1024,512]{1,0:T(8,128)(2,1)} collective-permute-done((bf16[1024,512]{1,0:T(8,128)(2,1)}, bf16[1024,512]{1,0:T(8,128)(2,1)}, u32[]{:S(2)}, u32[]{:S(2)}) %collective-permute-start.8) | collective-permute-done | bytes 1048608 | tf_op jit(solution)/shard_map/ppermute | solution.py:23
  297.9 2.8 fusion.40
  300.7 1.9 collective-permute-start.9
  302.6 1.9 collective-permute-start.10
  304.6 1.9 collective-permute-start.11
  306.5 4.4 %collective-permute-start.12 = (bf16[128,512]{1,0:T(8,128)(2,1)S(1)}, bf16[128,512]{1,0:T(8,128)(2,1)S(1)}, u32[]{:S(2)}, u32[]{:S(2)}) collective-permute-start(bf16[128,512]{1,0:T(8,128)(2,1)S(1)} %fusion.40), channel_id=1, source_target_pairs={{0,1},{1,2},{2,3},{3,4},{4,5},{5,6},{6,7},{7,8},{8,9},{9,10},{10,1... | collective-permute-start | bytes 393224 | tf_op jit(solution)/shard_map/ppermute | solution.py:34
  310.9 3.8 %convolution_convert_fusion = bf16[128,2048]{1,0:T(8,128)(2,1)} fusion(bf16[128,512]{0,1:T(8,128)(2,1)S(1)} %copy-done.25, bf16[1024,512]{1,0:T(8,128)(2,1)} %collective-permute-done.8, bf16[1024,512]{1,0:T(8,128)(2,1)} %maximum_select_fusion.1, pred[]{:T(512)S(6)} %eq.15), kind=kOutput, calls=%fused_computation.5 | convolution fusion | flops 278134784 | bytes 2752513 | tf_op jit(solution)/shard_map/dot_general | solution.py:123
  325.8 1.0 fusion.74
  326.9 1.9 collective-permute-start.13
  328.8 4.2 %collective-permute-start.14 = (f32[128,512]{0,1:T(8,128)}, f32[128,512]{0,1:T(8,128)S(1)}, u32[]{:S(2)}, u32[]{:S(2)}) collective-permute-start(f32[128,512]{0,1:T(8,128)} %get-tuple-element.45), channel_id=1, source_target_pairs={{2,0},{3,1},{4,2},{5,3},{6,4},{7,5},{8,6},{9,7},{10,8},{11,9},{12,... | collective-permute-start | bytes 786440 | tf_op jit(solution)/shard_map/ppermute | solution.py:34
  333.0 1.9 collective-permute-start.15
  334.9 1.9 collective-permute-start.16
  338.9 1.0 copy.197
  339.9 1.1 pad_maximum_fusion.2
  341.1 8.4 %collective-permute-done.14 = f32[128,512]{0,1:T(8,128)S(1)} collective-permute-done((f32[128,512]{0,1:T(8,128)}, f32[128,512]{0,1:T(8,128)S(1)}, u32[]{:S(2)}, u32[]{:S(2)}) %collective-permute-start.14) | collective-permute-done | bytes 262176 | tf_op jit(solution)/shard_map/ppermute | solution.py:34
  349.5 2.6 collective-permute-done.15
  352.1 2.7 collective-permute-done.16
  354.8 1.1 fusion.56
  (133 shorter events, 20.7 us)
Async XLA Ops:
  7.2 57.8 %copy-start = (bf16[128,2048]{1,0:T(8,128)(2,1)S(1)}, bf16[128,2048]{1,0:T(8,128)(2,1)}, u32[]{:S(2)}) copy-start(bf16[128,2048]{1,0:T(8,128)(2,1)} %param.7) | copy-start | bytes 1572868
  7.2 13.4 %copy-start.23 = (bf16[128,2048]{1,0:T(8,128)(2,1)S(1)}, bf16[128,2048]{1,0:T(8,128)(2,1)}, u32[]{:S(2)}) copy-start(bf16[128,2048]{1,0:T(8,128)(2,1)} %param.10) | copy-start | bytes 1572868
  7.2 195.3 %reduce-scatter.4.cloned.1.call-start = ((), (), s32[]{:S(2)}) async-start(), calls=%async_computation.1 | async-start | bytes 4325376 | tf_op jit(solution)/shard_map/reduce_scatter | solution.py:126
  7.2 15.9 %collective-permute-start = (bf16[128,512]{1,0:T(8,128)(2,1)}, bf16[128,512]{1,0:T(8,128)(2,1)S(1)}, u32[]{:S(2)}, u32[]{:S(2)}) collective-permute-start(bf16[128,512]{1,0:T(8,128)(2,1)} %param.9), channel_id=1, source_target_pairs={{0,4},{1,5},{2,6},{3,7},{4,8},{5,9},{6,10},{7,11},{8,12},{9,13},{1... | collective-permute-start | bytes 393224 | tf_op jit(solution)/shard_map/ppermute | solution.py:34
  10.8 12.4 %collective-permute-start.1 = (bf16[128,512]{1,0:T(8,128)(2,1)}, bf16[128,512]{1,0:T(8,128)(2,1)S(1)}, u32[]{:S(2)}, u32[]{:S(2)}) collective-permute-start(bf16[128,512]{1,0:T(8,128)(2,1)} %param.9), channel_id=1, source_target_pairs={{0,3},{1,4},{2,5},{3,6},{4,7},{5,8},{6,9},{7,10},{8,11},{9,12},{10... | collective-permute-start | bytes 393224 | tf_op jit(solution)/shard_map/ppermute | solution.py:34
  13.4 9.8 %collective-permute-start.2 = (bf16[128,512]{1,0:T(8,128)(2,1)}, bf16[128,512]{1,0:T(8,128)(2,1)S(1)}, u32[]{:S(2)}, u32[]{:S(2)}) collective-permute-start(bf16[128,512]{1,0:T(8,128)(2,1)} %param.9), channel_id=1, source_target_pairs={{0,2},{1,3},{2,4},{3,5},{4,6},{5,7},{6,8},{7,9},{8,10},{9,11},{10,... | collective-permute-start | bytes 393224 | tf_op jit(solution)/shard_map/ppermute | solution.py:34
  16.8 6.5 %collective-permute-start.3 = (bf16[128,512]{1,0:T(8,128)(2,1)}, bf16[128,512]{1,0:T(8,128)(2,1)S(1)}, u32[]{:S(2)}, u32[]{:S(2)}) collective-permute-start(bf16[128,512]{1,0:T(8,128)(2,1)} %param.9), channel_id=1, source_target_pairs={{0,1},{1,2},{2,3},{3,4},{4,5},{5,6},{6,7},{7,8},{8,9},{9,10},{10,1... | collective-permute-start | bytes 393224 | tf_op jit(solution)/shard_map/ppermute | solution.py:34
  20.9 2.4 copy-start.16
  21.1 12.0 %copy-start.20 = (bf16[128,512]{0,1:T(8,128)(2,1)}, bf16[128,512]{0,1:T(8,128)(2,1)S(1)}, u32[]{:S(2)}) copy-start(bf16[128,512]{0,1:T(8,128)(2,1)S(1)} %copy.198) | copy-start | bytes 393220
  21.1 2.2 copy-start.27
  21.2 3.8 %copy-start.12 = (bf16[128,512]{0,1:T(8,128)(2,1)}, bf16[128,512]{0,1:T(8,128)(2,1)S(1)}, u32[]{:S(2)}) copy-start(bf16[128,512]{0,1:T(8,128)(2,1)S(1)} %copy.273) | copy-start | bytes 393220
  22.1 4.3 %copy-start.8 = (bf16[128,512]{0,1:T(8,128)(2,1)}, bf16[128,512]{0,1:T(8,128)(2,1)S(1)}, u32[]{:S(2)}) copy-start(bf16[128,512]{0,1:T(8,128)(2,1)S(1)} %copy.274) | copy-start | bytes 393220
  23.1 13.1 %copy-start.10 = (bf16[128,512]{0,1:T(8,128)(2,1)}, bf16[128,512]{0,1:T(8,128)(2,1)S(1)}, u32[]{:S(2)}) copy-start(bf16[128,512]{0,1:T(8,128)(2,1)S(1)} %copy.210) | copy-start | bytes 393220
  23.3 1.6 copy-start.28
  26.4 7.0 %copy-start.5 = (f32[128,4,640]{0,2,1:T(8,128)}, f32[128,4,640]{0,2,1:T(8,128)S(1)}, u32[]{:S(2)}) copy-start(f32[128,4,640]{0,2,1:T(8,128)S(1)} %get-tuple-element.60) | copy-start | bytes 3932164
  33.1 0.9 copy-start.18
  33.5 1.3 copy-start.3
  34.0 1.0 copy-start.14
  34.8 1.3 copy-start.1
  36.8 10.1 %collective-permute-start.17 = (f32[128,512]{0,1:T(8,128)S(1)}, f32[128,512]{0,1:T(8,128)S(1)}, u32[]{:S(2)}, u32[]{:S(2)}) collective-permute-start(f32[128,512]{0,1:T(8,128)S(1)} %get-tuple-element.38), channel_id=1, source_target_pairs={{1,0},{2,1},{3,2},{4,3},{5,4},{6,5},{7,6},{8,7},{9,8},{10,9},{11,1... | collective-permute-start | bytes 786440 | tf_op jit(solution)/shard_map/ppermute | solution.py:34
  39.7 19.3 %collective-permute-start.18 = (f32[128,512]{0,1:T(8,128)S(1)}, f32[128,512]{0,1:T(8,128)S(1)}, u32[]{:S(2)}, u32[]{:S(2)}) collective-permute-start(f32[128,512]{0,1:T(8,128)S(1)} %get-tuple-element.41), channel_id=1, source_target_pairs={{2,0},{3,1},{4,2},{5,3},{6,4},{7,5},{8,6},{9,7},{10,8},{11,9},{12,... | collective-permute-start | bytes 786440 | tf_op jit(solution)/shard_map/ppermute | solution.py:34
  43.1 18.4 %collective-permute-start.19 = (f32[128,512]{0,1:T(8,128)S(1)}, f32[128,512]{0,1:T(8,128)S(1)}, u32[]{:S(2)}, u32[]{:S(2)}) collective-permute-start(f32[128,512]{0,1:T(8,128)S(1)} %get-tuple-element.40), channel_id=1, source_target_pairs={{3,0},{4,1},{5,2},{6,3},{7,4},{8,5},{9,6},{10,7},{11,8},{12,9},{13... | collective-permute-start | bytes 786440 | tf_op jit(solution)/shard_map/ppermute | solution.py:34
  45.0 19.2 %collective-permute-start.20 = (f32[128,512]{0,1:T(8,128)S(1)}, f32[128,512]{0,1:T(8,128)S(1)}, u32[]{:S(2)}, u32[]{:S(2)}) collective-permute-start(f32[128,512]{0,1:T(8,128)S(1)} %get-tuple-element.39), channel_id=1, source_target_pairs={{4,0},{5,1},{6,2},{7,3},{8,4},{9,5},{10,6},{11,7},{12,8},{13,9},{1... | collective-permute-start | bytes 786440 | tf_op jit(solution)/shard_map/ppermute | solution.py:34
  73.0 129.6 %copy-start.26 = (f32[64,512]{1,0:T(8,128)S(1)}, f32[64,512]{1,0:T(8,128)}, u32[]{:S(2)}) copy-start(f32[64,512]{1,0:T(8,128)} %param.11) | copy-start | bytes 393220
  204.4 1.3 collective-permute-start.4
  205.6 5.6 %copy-start.22 = (bf16[128,512]{1,0:T(8,128)(2,1)}, bf16[128,512]{1,0:T(8,128)(2,1)S(1)}, u32[]{:S(2)}) copy-start(bf16[128,512]{1,0:T(8,128)(2,1)S(1)} %maximum_select_fusion.6) | copy-start | bytes 393220
  205.7 9.5 %collective-permute-start.5 = (bf16[128,512]{1,0:T(8,128)(2,1)S(1)}, bf16[128,512]{1,0:T(8,128)(2,1)}, u32[]{:S(2)}, u32[]{:S(2)}) collective-permute-start(bf16[128,512]{1,0:T(8,128)(2,1)S(1)} %maximum_select_fusion.6), channel_id=1, source_target_pairs={{0,2},{1,3},{2,0},{3,1},{4,6},{5,7},{6,4},{7,5},{8,10},{9,11},{10,... | collective-permute-start | bytes 393224 | tf_op jit(solution)/shard_map/ppermute | solution.py:23
  216.3 16.7 %collective-permute-start.6 = (bf16[256,512]{1,0:T(8,128)(2,1)S(1)}, bf16[256,512]{1,0:T(8,128)(2,1)}, u32[]{:S(2)}, u32[]{:S(2)}) collective-permute-start(bf16[256,512]{1,0:T(8,128)(2,1)S(1)} %maximum_select_fusion.5), channel_id=1, source_target_pairs={{0,4},{1,5},{2,6},{3,7},{4,0},{5,1},{6,2},{7,3},{8,12},{9,13},{10,... | collective-permute-start | bytes 786440 | tf_op jit(solution)/shard_map/ppermute | solution.py:23
  234.9 13.1 %collective-permute-start.7 = (bf16[512,512]{1,0:T(8,128)(2,1)}, bf16[512,512]{1,0:T(8,128)(2,1)}, u32[]{:S(2)}, u32[]{:S(2)}) collective-permute-start(bf16[512,512]{1,0:T(8,128)(2,1)} %maximum_select_fusion.2), channel_id=1, source_target_pairs={{0,8},{1,9},{2,10},{3,11},{4,12},{5,13},{6,14},{7,15},{8,0},{9,1},... | collective-permute-start | bytes 1572872 | tf_op jit(solution)/shard_map/ppermute | solution.py:23
  251.0 46.9 %collective-permute-start.8 = (bf16[1024,512]{1,0:T(8,128)(2,1)}, bf16[1024,512]{1,0:T(8,128)(2,1)}, u32[]{:S(2)}, u32[]{:S(2)}) collective-permute-start(bf16[1024,512]{1,0:T(8,128)(2,1)} %maximum_select_fusion.1), channel_id=1, source_target_pairs={{0,16},{1,17},{2,18},{3,19},{4,20},{5,21},{6,22},{7,23},{8,24},{9,... | collective-permute-start | bytes 3145736 | tf_op jit(solution)/shard_map/ppermute | solution.py:23
  251.0 59.9 %copy-start.25 = (bf16[128,512]{0,1:T(8,128)(2,1)S(1)}, bf16[128,512]{0,1:T(8,128)(2,1)}, u32[]{:S(2)}) copy-start(bf16[128,512]{0,1:T(8,128)(2,1)} %copy-done.24) | copy-start | bytes 393220
  300.7 14.1 %collective-permute-start.9 = (bf16[128,512]{1,0:T(8,128)(2,1)S(1)}, bf16[128,512]{1,0:T(8,128)(2,1)S(1)}, u32[]{:S(2)}, u32[]{:S(2)}) collective-permute-start(bf16[128,512]{1,0:T(8,128)(2,1)S(1)} %fusion.40), channel_id=1, source_target_pairs={{0,4},{1,5},{2,6},{3,7},{4,8},{5,9},{6,10},{7,11},{8,12},{9,13},{1... | collective-permute-start | bytes 393224 | tf_op jit(solution)/shard_map/ppermute | solution.py:34
  302.6 12.1 %collective-permute-start.10 = (bf16[128,512]{1,0:T(8,128)(2,1)S(1)}, bf16[128,512]{1,0:T(8,128)(2,1)S(1)}, u32[]{:S(2)}, u32[]{:S(2)}) collective-permute-start(bf16[128,512]{1,0:T(8,128)(2,1)S(1)} %fusion.40), channel_id=1, source_target_pairs={{0,3},{1,4},{2,5},{3,6},{4,7},{5,8},{6,9},{7,10},{8,11},{9,12},{10... | collective-permute-start | bytes 393224 | tf_op jit(solution)/shard_map/ppermute | solution.py:34
  304.6 10.2 %collective-permute-start.11 = (bf16[128,512]{1,0:T(8,128)(2,1)S(1)}, bf16[128,512]{1,0:T(8,128)(2,1)S(1)}, u32[]{:S(2)}, u32[]{:S(2)}) collective-permute-start(bf16[128,512]{1,0:T(8,128)(2,1)S(1)} %fusion.40), channel_id=1, source_target_pairs={{0,2},{1,3},{2,4},{3,5},{4,6},{5,7},{6,8},{7,9},{8,10},{9,11},{10,... | collective-permute-start | bytes 393224 | tf_op jit(solution)/shard_map/ppermute | solution.py:34
  306.5 8.3 %collective-permute-start.12 = (bf16[128,512]{1,0:T(8,128)(2,1)S(1)}, bf16[128,512]{1,0:T(8,128)(2,1)S(1)}, u32[]{:S(2)}, u32[]{:S(2)}) collective-permute-start(bf16[128,512]{1,0:T(8,128)(2,1)S(1)} %fusion.40), channel_id=1, source_target_pairs={{0,1},{1,2},{2,3},{3,4},{4,5},{5,6},{6,7},{7,8},{8,9},{9,10},{10,1... | collective-permute-start | bytes 393224 | tf_op jit(solution)/shard_map/ppermute | solution.py:34
  314.7 1.2 copy-start.19
  314.9 1.5 copy-start.15
  316.0 1.4 copy-start.11
  316.4 2.0 copy-start.7
  318.3 0.9 copy-start.17
  318.3 1.3 copy-start.29
  319.2 1.4 copy-start.6
  321.5 1.3 copy-start.4
  323.7 1.3 copy-start.2
  326.9 14.2 %collective-permute-start.13 = (f32[128,512]{0,1:T(8,128)}, f32[128,512]{0,1:T(8,128)S(1)}, u32[]{:S(2)}, u32[]{:S(2)}) collective-permute-start(f32[128,512]{0,1:T(8,128)} %get-tuple-element.42), channel_id=1, source_target_pairs={{1,0},{2,1},{3,2},{4,3},{5,4},{6,5},{7,6},{8,7},{9,8},{10,9},{11,1... | collective-permute-start | bytes 786440 | tf_op jit(solution)/shard_map/ppermute | solution.py:34
  328.8 20.7 %collective-permute-start.14 = (f32[128,512]{0,1:T(8,128)}, f32[128,512]{0,1:T(8,128)S(1)}, u32[]{:S(2)}, u32[]{:S(2)}) collective-permute-start(f32[128,512]{0,1:T(8,128)} %get-tuple-element.45), channel_id=1, source_target_pairs={{2,0},{3,1},{4,2},{5,3},{6,4},{7,5},{8,6},{9,7},{10,8},{11,9},{12,... | collective-permute-start | bytes 786440 | tf_op jit(solution)/shard_map/ppermute | solution.py:34
  333.0 19.1 %collective-permute-start.15 = (f32[128,512]{0,1:T(8,128)}, f32[128,512]{0,1:T(8,128)}, u32[]{:S(2)}, u32[]{:S(2)}) collective-permute-start(f32[128,512]{0,1:T(8,128)} %get-tuple-element.44), channel_id=1, source_target_pairs={{3,0},{4,1},{5,2},{6,3},{7,4},{8,5},{9,6},{10,7},{11,8},{12,9},{13... | collective-permute-start | bytes 786440 | tf_op jit(solution)/shard_map/ppermute | solution.py:34
  334.9 19.8 %collective-permute-start.16 = (f32[128,512]{0,1:T(8,128)}, f32[128,512]{0,1:T(8,128)}, u32[]{:S(2)}, u32[]{:S(2)}) collective-permute-start(f32[128,512]{0,1:T(8,128)} %get-tuple-element.43), channel_id=1, source_target_pairs={{4,0},{5,1},{6,2},{7,3},{8,4},{9,5},{10,6},{11,7},{12,8},{13,9},{1... | collective-permute-start | bytes 786440 | tf_op jit(solution)/shard_map/ppermute | solution.py:34
  (4 other events, 3.4 us)
Sparse Core Ops, SparseCore 0:
  73.1 129.3 reduce-scatter.3
